TPU v7x, 32 devices: a whole 2x2x4 slice. The times are simulated.
32 devices in a mesh: groups: 2 (over x), ctx: 16 (over z, y, core).
Axes of the slice: x: 2, y: 2, z: 4, core: 2. Of those that a mesh axis runs over, the one named last changes fastest.
Arguments:
- inputs: bfloat16 [4096, 8192], P(None, ('groups', 'ctx')), parts along dimension 1, may hold values from -4 to 4
- projections: bfloat16 [512, 8192], P(None, ('groups', 'ctx')), parts along dimension 1, may hold values from -7 to 7
- step_sizes: bfloat16 [64, 8192], P(None, ('groups', 'ctx')), parts along dimension 1, may hold values from 0.0019989014 to 0.019897461
- log_rates: float32 [64], replicated, may hold values from -12 to 3
- skip_gain: float32 [64], replicated, may hold values from 0.5 to 1.5
- packing: int32 [32, 256], P(('groups', 'ctx')), parts along dimension 0, may hold values from 0 to 255, as said below
- prompt_sizes: int32 [8], P('groups'), parts along dimension 0, may hold values from 1 to 3072, 4096 in all
Outputs:
- ssd_output: bfloat16 [4096, 8192], P(None, ('groups', 'ctx')), parts along dimension 1
There are 2 independent parts, one for each index of `groups`. A program takes and returns all parts, laid end to end along the dimension named above; an argument that names none is the same for every part. Nothing has to cross between parts.
Inputs may be any that keep to these rules, and one draw needn't show every extreme that they name: `packing`: each row names every one of the loader's 256 tokens once. `prompt_sizes`: the lengths add up to 4096.
All inputs are finite; a program needn't handle non-finite values.
Results may differ from a plain program's by a relative error of at most 0.001.
The roundings to bfloat16 on the way count: a program that leaves them out, or rounds other values in their place, can miss the bound.
Values may be sent and summed in bfloat16 or wider, within the bound.
A program may use at most 320 MiB of HBM per device.

v0:
```python
import jax
import jax.numpy as jnp
from jax import lax
from jax.sharding import PartitionSpec as P

G = 4
BLOCK = 128


def carried_in(value, axis, join, neutral):
    count, mine = (lax.axis_size(axis), lax.axis_index(axis))
    pieces = jax.tree.map(lambda part: lax.all_gather(part, axis), value)
    so_far = jax.tree.map(
        lambda part, zero: jnp.full_like(part, 0) + jnp.asarray(zero, part.dtype), value, neutral
    )

    def lap(position, so_far):
        longer = join(so_far, jax.tree.map(lambda part: part[position], pieces))
        return jax.tree.map(lambda new, old: jnp.where(position < mine, new, old), longer, so_far)

    return lax.fori_loop(0, count - 1, lap, so_far)


def block_setup(block_dt, resets, decay_rate):
    step_size = block_dt.astype(jnp.float32)
    log_decay = jnp.cumsum(step_size * decay_rate[:, None], axis=1)
    before_reset = jnp.cumsum(resets) == 0
    return (step_size, log_decay, before_reset)


def block_state(block_x, block_bc, segment, setup):
    step_size, log_decay, before_reset = setup
    head_count = log_decay.shape[0]
    length = block_x.shape[1]
    per_group = head_count // G
    x_heads = block_x.reshape(G, per_group, -1, length)
    maps = block_bc.reshape(G, 2, -1, length)
    last_decay = log_decay[:, -1:]
    into_end = (
        jnp.where((segment == segment[-1])[None, :], jnp.exp(last_decay - log_decay), 0.0)
        * step_size
    )
    weighted = (x_heads * into_end.reshape(G, per_group, 1, length)).astype(jnp.bfloat16)
    block_total = jnp.einsum(
        "ghpj,gnj->ghpn", weighted, maps[:, 0], preferred_element_type=jnp.float32
    )
    block_keep = jnp.where(before_reset[-1], jnp.exp(last_decay[:, 0]), 0.0)
    return (block_keep, block_total.reshape(head_count, x_heads.shape[2], maps.shape[2]))


def block_output(block_x, block_bc, segment, setup, skip_gain, carry_in):
    step_size, log_decay, before_reset = setup
    head_count = log_decay.shape[0]
    length = block_x.shape[1]
    per_group = head_count // G
    head_width = block_x.shape[0] // head_count
    states = block_bc.shape[0] // (2 * G)
    column_index = jnp.arange(length, dtype=jnp.int32)
    allowed = (column_index[:, None] >= column_index[None, :]) & (
        segment[:, None] == segment[None, :]
    )

    def group_part(operands):
        x_group, map_group, step_group, decay_group, carry_group, skip_group = operands
        x_heads = x_group.reshape(per_group, head_width, length)
        input_map = map_group[0]
        output_map = map_group[1]
        decay_gap = decay_group[:, :, None] - decay_group[:, None, :]
        decay_mask = jnp.exp(jnp.where(allowed[None], decay_gap, -jnp.inf))
        inner_gram = jnp.einsum(
            "ni,nj->ij", output_map, input_map, preferred_element_type=jnp.float32
        )
        mixing = (inner_gram[None] * (decay_mask * step_group[:, None, :])).astype(jnp.bfloat16)
        within = jnp.einsum("hij,hpj->hpi", mixing, x_heads, preferred_element_type=jnp.float32)
        opened = jnp.where(before_reset[None, :], jnp.exp(decay_group), 0.0)
        carried = jnp.einsum(
            "hpn,ni->hpi",
            carry_group.astype(jnp.bfloat16),
            output_map,
            preferred_element_type=jnp.float32,
        )
        result = (
            within
            + carried * opened[:, None, :]
            + skip_group[:, None, None] * x_heads.astype(jnp.float32)
        )
        return result.reshape(-1, length).astype(jnp.bfloat16)

    grouped = (
        block_x.reshape(G, -1, length),
        block_bc.reshape(G, 2, states, length),
        step_size.reshape(G, per_group, length),
        log_decay.reshape(G, per_group, length),
        carry_in.reshape(G, per_group, head_width, states),
        skip_gain.reshape(G, per_group),
    )
    outputs = lax.map(group_part, grouped)
    return outputs.reshape(-1, length)


def combine(earlier, later):
    return (earlier[0] * later[0], later[0][:, None, None] * earlier[1] + later[1])


def per_device(inputs, projections, step_sizes, log_rates, skip_gain, packing, prompt_sizes):
    own_rows = inputs.shape[1]
    head_count = log_rates.shape[0]
    states = projections.shape[0] // (2 * G)
    head_width = inputs.shape[0] // head_count
    send_order = packing[0]
    owned_x, owned_bc, owned_dt = (
        lax.all_to_all(
            jnp.take(inputs, send_order, axis=1), "ctx", split_axis=1, concat_axis=1, tiled=True
        ),
        lax.all_to_all(
            jnp.take(projections, send_order, axis=1),
            "ctx",
            split_axis=1,
            concat_axis=1,
            tiled=True,
        ),
        lax.all_to_all(
            jnp.take(step_sizes, send_order, axis=1), "ctx", split_axis=1, concat_axis=1, tiled=True
        ),
    )
    position = lax.axis_index("ctx") * own_rows + jnp.arange(own_rows, dtype=jnp.int32)
    prompt_start = jnp.cumsum(prompt_sizes) - prompt_sizes
    segment = jnp.sum((position[:, None] >= prompt_start[None, :]).astype(jnp.int32), axis=1) - 1
    resets = jnp.sum((position[:, None] == prompt_start[None, :]).astype(jnp.int32), axis=1)
    decay_rate = -jnp.exp(log_rates)
    block_count = own_rows // BLOCK
    setups = []
    keeps = []
    totals = []
    dev_keep = jnp.ones((head_count,), jnp.float32)
    dev_total = jnp.zeros((head_count, head_width, states), jnp.float32)
    for block_id in range(block_count):
        lower = block_id * BLOCK
        upper = lower + BLOCK
        setup = block_setup(owned_dt[:, lower:upper], resets[lower:upper], decay_rate)
        block_keep, block_total = block_state(
            owned_x[:, lower:upper], owned_bc[:, lower:upper], segment[lower:upper], setup
        )
        setups.append(setup)
        keeps.append(block_keep)
        totals.append(block_total)
        dev_total = block_keep[:, None, None] * dev_total + block_total
        dev_keep = dev_keep * block_keep
    identity = (
        jnp.ones((head_count,), jnp.float32),
        jnp.zeros((head_count, head_width, states), jnp.float32),
    )
    carry_in = carried_in((dev_keep, dev_total), "ctx", combine, identity)[1]
    results = []
    for block_id in range(block_count):
        lower = block_id * BLOCK
        upper = lower + BLOCK
        results.append(
            block_output(
                owned_x[:, lower:upper],
                owned_bc[:, lower:upper],
                segment[lower:upper],
                setups[block_id],
                skip_gain,
                carry_in,
            )
        )
        carry_in = keeps[block_id][:, None, None] * carry_in + totals[block_id]
    return jnp.concatenate(results, axis=1)


def solution(mesh):
    in_specs = (
        P(None, ("groups", "ctx")),
        P(None, ("groups", "ctx")),
        P(None, ("groups", "ctx")),
        P(),
        P(),
        P(("groups", "ctx"), None),
        P("groups"),
    )
    out_specs = P(None, ("groups", "ctx"))
    return jax.shard_map(
        per_device, mesh=mesh, in_specs=in_specs, out_specs=out_specs, check_vma=False
    )
```

profile of v0, /device:TPU:0, one launch (start us, length us, event | category | flops | bytes accessed | tf_op | source)
XLA Modules:
  0.0 353.7 jit_solution(8487469282059257848)
XLA Ops:
  8.6 1.3 reduce.11
  11.7 7.4 %all-to-all-start.2 = ((bf16[16,2,512]{2,1,0:T(2,128)(2,1)}), bf16[16,2,512]{2,1,0:T(2,128)(2,1)S(1)}, u32[]{:S(2)}, u32[]{:S(2)}) async-start(bf16[16,2,512]{2,1,0:T(2,128)(2,1)} %reshape.453), calls=%async_computation.2 | async-start | bytes 65536 | tf_op jit(solution)/shard_map/all_to_all | solution.py:122
  20.2 1.2 gather_fusion.1
  22.2 2.9 copy.56
  25.1 3.2 gather_fusion
  28.3 6.0 %all-to-all-start.1 = ((bf16[512,16,16]{0,2,1:T(8,128)(2,1)}), bf16[512,16,16]{0,2,1:T(8,128)(2,1)S(1)}, u32[]{:S(2)}, u32[]{:S(2)}) async-start(bf16[512,16,16]{0,2,1:T(8,128)(2,1)} %broadcast_select_fusion.1), calls=%async_computation.1 | async-start | bytes 524288 | tf_op jit(solution)/shard_map/all_to_all | solution.py:115
  34.3 3.2 broadcast_select_fusion
  37.5 6.8 %all-to-all-done.1 = bf16[512,16,16]{0,2,1:T(8,128)(2,1)S(1)} async-done(((bf16[512,16,16]{0,2,1:T(8,128)(2,1)}), bf16[512,16,16]{0,2,1:T(8,128)(2,1)S(1)}, u32[]{:S(2)}, u32[]{:S(2)}) %all-to-all-start.1) | async-done | bytes 262176 | tf_op jit(solution)/shard_map/all_to_all | solution.py:115
  44.3 3.7 %all-to-all-start = ((bf16[4096,16,16]{0,2,1:T(8,128)(2,1)}), bf16[4096,16,16]{0,2,1:T(8,128)(2,1)S(1)}, u32[]{:S(2)}, u32[]{:S(2)}) async-start(bf16[4096,16,16]{0,2,1:T(8,128)(2,1)} %broadcast_select_fusion), calls=%async_computation | async-start | bytes 4194304 | tf_op jit(solution)/shard_map/all_to_all | solution.py:112
  50.9 1.2 broadcast_compare_fusion.2
  53.1 2.0 slice_reduce_fusion
  55.1 1.2 broadcast_select_fusion.4
  56.3 1.3 broadcast_multiply_fusion.1
  58.6 30.3 %all-to-all-done = bf16[4096,16,16]{0,2,1:T(8,128)(2,1)S(1)} async-done(((bf16[4096,16,16]{0,2,1:T(8,128)(2,1)}), bf16[4096,16,16]{0,2,1:T(8,128)(2,1)S(1)}, u32[]{:S(2)}, u32[]{:S(2)}) %all-to-all-start) | async-done | bytes 2097184 | tf_op jit(solution)/shard_map/all_to_all | solution.py:112
  89.0 1.1 fusion.60
  93.7 1.6 bitcast_add_fusion.2
  98.2 41.0 %all-reduce = f32[1024]{0:T(1024)S(1)} all-reduce(f32[1024]{0:T(1024)S(1)} %dynamic-update-slice), channel_id=2, replica_groups=mesh['groups'=2,'ctx'=16] {'ctx'}, use_global_device_ids=true, to_apply=%add | all-reduce | flops 1024 | bytes 8192
  140.4 130.0 %all-gather.3.cloned.1.call-done = f32[16,64,64,64]{3,2,1,0:T(8,128)} async-done(((f32[1,64,64,64]{3,2,1,0:T(8,128)}), f32[16,64,64,64]{3,2,1,0:T(8,128)}) %all-gather.3.cloned.1.call-update) | async-done | bytes 16777232 | tf_op jit(solution)/shard_map/all_gather | solution.py:12
  270.4 41.8 %while.38 = (s32[]{:T(128)}, f32[64,64,64]{2,1,0:T(8,128)S(1)}, s32[]{:T(128)}, f32[16,64]{1,0:T(8,128)}, f32[16,64,64,64]{3,2,1,0:T(8,128)}, /*index=5*/s32[]{:T(128)}, s32[]{:T(128)}) while((s32[]{:T(128)}, f32[64,64,64]{2,1,0:T(8,128)S(1)}, s32[]{:T(128)}, f32[16,64]{1,0:T(8,128)}, f32[16,64,64,64]{3,2,1,0:T(8,128)}, ...), condition=%wide.region_8.9_spmd.clone, body=%wide.region_7.8_spmd.clone.sunk | while | flops 1048580 | bytes 3146601 | solution.py:21
  271.1 2.1 fusion.105
  273.9 2.1 fusion.105
  276.7 2.1 fusion.105
  279.5 2.1 fusion.105
  282.3 2.1 fusion.105
  285.0 2.1 fusion.105
  287.8 2.1 fusion.105
  290.6 2.1 fusion.105
  293.4 2.1 fusion.105
  296.2 2.1 fusion.105
  299.0 2.1 fusion.105
  301.8 2.1 fusion.105
  304.6 2.1 fusion.105
  307.3 2.1 fusion.105
  310.1 2.1 fusion.105
  312.2 1.2 convert.26
  313.4 1.2 broadcast.157.clone.1
  314.6 17.8 %while.36 = (s32[]{:T(128)}, bf16[4,1024,128]{2,1,0:T(8,128)(2,1)}, bf16[4,1024,128]{2,1,0:T(8,128)(2,1)}, bf16[4,2,64,128]{3,2,1,0:T(8,128)(2,1)S(1)}, f32[4,16...) while((s32[]{:T(128)}, bf16[4,1024,128]{2,1,0:T(8,128)(2,1)}, ...), condition=%wide.region_10.11_spmd.clone, body=%wide.region_9.10_spmd.clone.sunk | while | flops 54577152 | bytes 3428257 | solution.py:97
  317.1 1.2 fusion.95
  321.6 1.2 fusion.95
  326.1 1.2 fusion.95
  330.5 1.2 fusion.95
  332.4 2.9 bitcast_add_fusion.1
  335.4 8.6 %while.37 = (s32[]{:T(128)}, bf16[4,1024,128]{2,1,0:T(8,128)(2,1)S(1)}, bf16[4,1024,128]{2,1,0:T(8,128)(2,1)S(1)}, bf16[4,2,64,128]{3,2,1,0:T(8,128)(2,1)S(1)}, ...) while((s32[]{:T(128)}, ...), condition=%wide.region_12.13_spmd.clone, body=%wide.region_11.12_spmd.clone.sunk | while | flops 54577152 | bytes 3427749 | solution.py:97
  336.4 1.2 fusion.104
  338.5 1.2 fusion.104
  340.7 1.2 fusion.104
  342.9 1.2 fusion.104
  344.1 2.8 pad_maximum_fusion
  (164 shorter events, 44.7 us)
Async XLA Ops:
  11.7 16.6 %all-to-all-start.2 = ((bf16[16,2,512]{2,1,0:T(2,128)(2,1)}), bf16[16,2,512]{2,1,0:T(2,128)(2,1)S(1)}, u32[]{:S(2)}, u32[]{:S(2)}) async-start(bf16[16,2,512]{2,1,0:T(2,128)(2,1)} %reshape.453), calls=%async_computation.2 | async-start | bytes 65536 | tf_op jit(solution)/shard_map/all_to_all | solution.py:122
  28.3 16.0 %all-to-all-start.1 = ((bf16[512,16,16]{0,2,1:T(8,128)(2,1)}), bf16[512,16,16]{0,2,1:T(8,128)(2,1)S(1)}, u32[]{:S(2)}, u32[]{:S(2)}) async-start(bf16[512,16,16]{0,2,1:T(8,128)(2,1)} %broadcast_select_fusion.1), calls=%async_computation.1 | async-start | bytes 524288 | tf_op jit(solution)/shard_map/all_to_all | solution.py:115
  37.5 10.6 %copy-start.12 = (s32[4]{0:T(128)S(1)}, s32[4]{0:T(128)}, u32[]{:S(2)}) copy-start(s32[4]{0:T(128)} %param.19) | copy-start | bytes 52
  37.5 13.4 %copy-start.13 = (f32[64]{0:T(128)S(1)}, f32[64]{0:T(128)}, u32[]{:S(2)}) copy-start(f32[64]{0:T(128)} %param.16) | copy-start | bytes 772
  44.3 44.6 %all-to-all-start = ((bf16[4096,16,16]{0,2,1:T(8,128)(2,1)}), bf16[4096,16,16]{0,2,1:T(8,128)(2,1)S(1)}, u32[]{:S(2)}, u32[]{:S(2)}) async-start(bf16[4096,16,16]{0,2,1:T(8,128)(2,1)} %broadcast_select_fusion), calls=%async_computation | async-start | bytes 4194304 | tf_op jit(solution)/shard_map/all_to_all | solution.py:112
  48.0 222.4 %all-gather.3.cloned.1.call-start = ((), (), s32[]{:S(2)}) async-start(), calls=%async_computation.3 | async-start | bytes 35651584 | tf_op jit(solution)/shard_map/all_gather | solution.py:12
  50.2 0.7 copy-start.4
  90.1 1.2 copy-start.2
  90.7 1.7 copy-start.1
  91.9 0.8 copy-start.3
  92.4 1.3 copy-start
  92.4 1.3 copy-start.8
  92.4 1.3 copy-start.11
  95.4 0.7 copy-start.10
  95.4 1.3 copy-start.14
  95.4 2.5 copy-start.5
  95.4 2.5 copy-start.9
  312.2 2.4 copy-start.6
  314.6 17.8 %copy-start.7 = (f32[64]{0:T(128)S(1)}, f32[64]{0:T(128)}, u32[]{:S(2)}) copy-start(f32[64]{0:T(128)} %get-tuple-element.354) | copy-start | bytes 772
Sparse Core Ops, SparseCore 0:
  95.5 174.8 all-gather.2
where the time goes:
time: 356 us; the launch traced here: 354 us
  waiting for transfers between devices  167 us (47%)
  other arithmetic  54.9 us (15%)
  local copies, waits for them, and re-layouts  42.3 us (12%)
  blocking collectives  41 us (12%)
  starting transfers between devices  17.2 us (5%)
  matrix products  16 us (4%)
  between operations  14.3 us (4%)
    all_gather x1, waiting for transfers between devices, carried_in(): pieces = jax.tree.map(lambda part: lax.all_gather(part, axis), value)  130 us
    unnamed x1, blocking collectives  41 us
    select_n x15, other arithmetic, lap(): jnp.where(position < mine, new, old)  31.1 us
    all_to_all x1, waiting for transfers between devices, per_device(): lax.all_to_all(jnp.take(inputs, send_order, axis=1), 'ctx', split_axis=1,...  30.3 us
    unnamed x43, local copies, waits for them, and re-layouts  10.6 us
    mul x15, local copies, waits for them, and re-layouts, combine(): later[0][:, None, None] * earlier[1] + later[1]  10.4 us
    dot_general x8, matrix products, group_part(): jnp.einsum('hpn,ni->hpi', carry_group.astype(jnp.bfloat16), output_map, p...  9.35 us
    all_to_all x1, starting transfers between devices, per_device(): lax.all_to_all(jnp.take(step_sizes, send_order, axis=1), 'ctx', split_axi...  7.41 us
  transfers between devices with their start and end apart: 4, of which 3 were waited for; matrix products, arithmetic and copies ran while one was open for 7% of the time, Pallas kernels for 0%

commit v1 on v0

--- a/solution.py
+++ b/solution.py
@@ -5,6 +5,22 @@
 
 G = 4
 BLOCK = 128
+
+
+def pairwise_exchange(x, axis, split, join):
+    ways, here = (lax.axis_size(axis), lax.axis_index(axis))
+    width = x.shape[split] // ways
+    shape = list(x.shape)
+    shape[split] = width
+    height = shape[join]
+    shape[join] = height * ways
+    full = jnp.zeros(shape, x.dtype)
+    for mask in range(ways):
+        part = lax.dynamic_slice_in_dim(x, (here ^ mask) * width, width, axis=split)
+        if mask:
+            part = lax.ppermute(part, axis, [(d, d ^ mask) for d in range(ways)])
+        full = lax.dynamic_update_slice_in_dim(full, part, (here ^ mask) * height, axis=join)
+    return full
 
 
 def carried_in(value, axis, join, neutral):
@@ -109,9 +125,7 @@
     head_width = inputs.shape[0] // head_count
     send_order = packing[0]
     owned_x, owned_bc, owned_dt = (
-        lax.all_to_all(
-            jnp.take(inputs, send_order, axis=1), "ctx", split_axis=1, concat_axis=1, tiled=True
-        ),
+        pairwise_exchange(jnp.take(inputs, send_order, axis=1), "ctx", 1, 1),
         lax.all_to_all(
             jnp.take(projections, send_order, axis=1),
             "ctx",

time: 356 us -> 388 us (1.090)
  local copies, waits for them, and re-layouts: 42.3 us -> 82.8 us
  starting transfers between devices: 17.2 us -> 38 us
  waiting for transfers between devices: 167 us -> 149 us
  blocking collectives: 41 us -> 33.5 us
    dynamic_update_slice x0 -> x17, local copies, waits for them, and re-layouts: none -> 39.4 us  [pairwise_exchange(): lax.dynamic_update_slice_in_dim(full, part, (here ^ mask) * height, axis=...]
    all_to_all x1 -> x0, waiting for transfers between devices: 30.3 us -> none  [per_device(): lax.all_to_all(jnp.take(inputs, send_order, axis=1), 'ctx', split_axis=1,...]
    ppermute x0 -> x15, starting transfers between devices: none -> 25.9 us  [pairwise_exchange(): part = lax.ppermute(part, axis, [(d, d ^ mask) for d in range(ways)])]
    ppermute x0 -> x15, waiting for transfers between devices: none -> 10.9 us  [pairwise_exchange(): part = lax.ppermute(part, axis, [(d, d ^ mask) for d in range(ways)])]
    all_gather x1, waiting for transfers between devices: 130 us -> 138 us  [carried_in(): pieces = jax.tree.map(lambda part: lax.all_gather(part, axis), value)]
    unnamed x1, blocking collectives: 41 us -> 33.5 us
    all_to_all x1, waiting for transfers between devices: 6.84 us -> 0.01 us  [per_device(): lax.all_to_all(jnp.take(projections, send_order, axis=1), 'ctx', split_ax...]
    unnamed x43 -> x37, local copies, waits for them, and re-layouts: 10.6 us -> 9.01 us
  transfers between devices with their start and end apart: 4 -> 18, of which waited for: 3 -> 3; matrix products, arithmetic and copies ran while one was open for 7% -> 15% of each run, Pallas kernels for 0% -> 0%
where the time goes in v1:
time: 388 us; the launch traced here: 385 us
  waiting for transfers between devices  149 us (38%)
  local copies, waits for them, and re-layouts  82.8 us (21%)
  other arithmetic  51.2 us (13%)
  starting transfers between devices  38 us (10%)
  blocking collectives  33.5 us (9%)
  matrix products  16 us (4%)
  between operations  14.4 us (4%)
    all_gather x1, waiting for transfers between devices, carried_in(): pieces = jax.tree.map(lambda part: lax.all_gather(part, axis), value)  138 us
    dynamic_update_slice x17, local copies, waits for them, and re-layouts, pairwise_exchange(): lax.dynamic_update_slice_in_dim(full, part, (here ^ mask) * height, axis=...  39.4 us
    unnamed x1, blocking collectives  33.5 us
    select_n x15, other arithmetic, lap(): jnp.where(position < mine, new, old)  31.1 us
    ppermute x15, starting transfers between devices, pairwise_exchange(): part = lax.ppermute(part, axis, [(d, d ^ mask) for d in range(ways)])  25.9 us
    ppermute x15, waiting for transfers between devices, pairwise_exchange(): part = lax.ppermute(part, axis, [(d, d ^ mask) for d in range(ways)])  10.9 us
    mul x15, local copies, waits for them, and re-layouts, combine(): later[0][:, None, None] * earlier[1] + later[1]  10.3 us
    dot_general x8, matrix products, group_part(): jnp.einsum('hpn,ni->hpi', carry_group.astype(jnp.bfloat16), output_map, p...  9.35 us
  transfers between devices with their start and end apart: 18, of which 3 were waited for; matrix products, arithmetic and copies ran while one was open for 15% of the time, Pallas kernels for 0%

profile of v1, /device:TPU:0, one launch (start us, length us, event | category | flops | bytes accessed | tf_op | source)
XLA Modules:
  0.0 385.3 jit_solution(63622977947277200)
XLA Ops:
  7.2 2.9 copy.60
  10.3 3.2 gather_fusion
  13.4 1.8 broadcast_select_fusion
  17.0 2.5 collective-permute-start.1
  19.6 1.8 collective-permute-start.3
  24.5 6.1 %all-to-all-start.1 = ((bf16[16,2,512]{2,1,0:T(2,128)(2,1)}), bf16[16,2,512]{2,1,0:T(2,128)(2,1)S(1)}, u32[]{:S(2)}, u32[]{:S(2)}) async-start(bf16[16,2,512]{2,1,0:T(2,128)(2,1)} %reshape.446), calls=%async_computation.1 | async-start | bytes 65536 | tf_op jit(solution)/shard_map/all_to_all | solution.py:136
  38.3 6.0 %all-to-all-start = ((bf16[512,16,16]{0,2,1:T(8,128)(2,1)}), bf16[512,16,16]{0,2,1:T(8,128)(2,1)S(1)}, u32[]{:S(2)}, u32[]{:S(2)}) async-start(bf16[512,16,16]{0,2,1:T(8,128)(2,1)} %broadcast_select_fusion.1), calls=%async_computation | async-start | bytes 524288 | tf_op jit(solution)/shard_map/all_to_all | solution.py:129
  48.8 2.9 collective-permute-start.5
  51.7 1.6 constant_dynamic-update-slice_fusion.12
  53.3 1.6 constant_dynamic-update-slice_fusion.11
  54.8 2.4 collective-permute-start.7
  57.2 1.6 constant_dynamic-update-slice_fusion.10
  59.1 1.6 constant_dynamic-update-slice_fusion.9
  60.6 3.5 collective-permute-start.9
  64.2 1.6 constant_dynamic-update-slice_fusion.8
  66.4 3.3 collective-permute-start.11
  70.3 6.1 %collective-permute-done.7 = bf16[4096,16]{0,1:T(8,128)(2,1)S(1)} collective-permute-done((bf16[4096,16]{0,1:T(8,128)(2,1)}, bf16[4096,16]{0,1:T(8,128)(2,1)S(1)}, u32[]{:S(2)}, u32[]{:S(2)}) %collective-permute-start.7) | collective-permute-done | bytes 131104 | tf_op jit(solution)/shard_map/ppermute | solution.py:21
  76.4 2.6 collective-permute-start.12
  79.7 3.3 collective-permute-start.13
  83.7 4.8 %collective-permute-done.9 = bf16[4096,16]{0,1:T(8,128)(2,1)S(1)} collective-permute-done((bf16[4096,16]{0,1:T(8,128)(2,1)S(1)}, bf16[4096,16]{0,1:T(8,128)(2,1)S(1)}, u32[]{:S(2)}, u32[]{:S(2)}) %collective-permute-start.9) | collective-permute-done | bytes 131104 | tf_op jit(solution)/shard_map/ppermute | solution.py:21
  88.5 2.7 collective-permute-start.14
  93.8 4.1 %copy.61 = bf16[4096,256]{1,0:T(8,128)(2,1)} copy(bf16[4096,256]{0,1:T(8,128)(2,1)} %constant_dynamic-update-slice_fusion) | data formatting | bytes 4194304 | tf_op jit(solution)/shard_map/dynamic_update_slice | solution.py:22
  98.4 11.1 %dynamic_update_slice.69 = bf16[4096,256]{1,0:T(8,128)(2,1)} dynamic-update-slice(bf16[4096,256]{1,0:T(8,128)(2,1)} %copy.61, bf16[4096,16]{1,0:T(8,128)(2,1)S(1)} %copy.62, s32[]{:T(128)} %constant.135.clone.1, s32[]{:T(128)S(6)} %select_n.215) | dynamic-update-slice | bytes 262148 | tf_op jit(solution)/shard_map/dynamic_update_slice | solution.py:22
  109.9 11.1 %dynamic_update_slice.70 = bf16[4096,256]{1,0:T(8,128)(2,1)} dynamic-update-slice(bf16[4096,256]{1,0:T(8,128)(2,1)} %dynamic_update_slice.69, bf16[4096,16]{1,0:T(8,128)(2,1)S(1)} %copy.63, s32[]{:T(128)} %constant.135.clone.1, s32[]{:T(128)S(6)} %select_n.216) | dynamic-update-slice | bytes 262148 | tf_op jit(solution)/shard_map/dynamic_update_slice | solution.py:22
  121.0 1.7 fusion.60
  125.4 1.7 bitcast_add_fusion.2
  129.8 33.5 %all-reduce = f32[1024]{0:T(1024)S(1)} all-reduce(f32[1024]{0:T(1024)S(1)} %dynamic-update-slice), channel_id=2, replica_groups=mesh['groups'=2,'ctx'=16] {'ctx'}, use_global_device_ids=true, to_apply=%add | all-reduce | flops 1024 | bytes 8192
  164.5 137.7 %all-gather.3.cloned.1.call-done = f32[16,64,64,64]{3,2,1,0:T(8,128)} async-done(((f32[1,64,64,64]{3,2,1,0:T(8,128)}), f32[16,64,64,64]{3,2,1,0:T(8,128)}) %all-gather.3.cloned.1.call-update) | async-done | bytes 16777232 | tf_op jit(solution)/shard_map/all_gather | solution.py:28
  302.2 41.7 %while.38 = (s32[]{:T(128)}, f32[64,64,64]{2,1,0:T(8,128)S(1)}, s32[]{:T(128)}, f32[16,64]{1,0:T(8,128)}, f32[16,64,64,64]{3,2,1,0:T(8,128)}, /*index=5*/s32[]{:T(128)}, s32[]{:T(128)}) while((s32[]{:T(128)}, f32[64,64,64]{2,1,0:T(8,128)S(1)}, s32[]{:T(128)}, f32[16,64]{1,0:T(8,128)}, f32[16,64,64,64]{3,2,1,0:T(8,128)}, ...), condition=%wide.region_8.9_spmd.clone, body=%wide.region_7.8_spmd.clone.sunk | while | flops 1048580 | bytes 3146601 | solution.py:37
  302.9 2.1 fusion.105
  305.7 2.1 fusion.105
  308.5 2.1 fusion.105
  311.2 2.1 fusion.105
  314.0 2.1 fusion.105
  316.8 2.1 fusion.105
  319.6 2.1 fusion.105
  322.4 2.1 fusion.105
  325.1 2.1 fusion.105
  327.9 2.1 fusion.105
  330.7 2.1 fusion.105
  333.5 2.1 fusion.105
  336.3 2.1 fusion.105
  339.1 2.1 fusion.105
  341.9 2.1 fusion.105
  346.3 17.8 %while.36 = (s32[]{:T(128)}, bf16[4,1024,128]{2,1,0:T(8,128)(2,1)}, bf16[4,1024,128]{2,1,0:T(8,128)(2,1)}, bf16[4,2,64,128]{3,2,1,0:T(8,128)(2,1)S(1)}, f32[4,16...) while((s32[]{:T(128)}, bf16[4,1024,128]{2,1,0:T(8,128)(2,1)}, ...), condition=%wide.region_10.11_spmd.clone, body=%wide.region_9.10_spmd.clone.sunk | while | flops 54577152 | bytes 3428257 | solution.py:113
  364.1 2.9 bitcast_add_fusion.1
  367.1 8.6 %while.37 = (s32[]{:T(128)}, bf16[4,1024,128]{2,1,0:T(8,128)(2,1)S(1)}, bf16[4,1024,128]{2,1,0:T(8,128)(2,1)S(1)}, bf16[4,2,64,128]{3,2,1,0:T(8,128)(2,1)S(1)}, ...) while((s32[]{:T(128)}, ...), condition=%wide.region_12.13_spmd.clone, body=%wide.region_11.12_spmd.clone.sunk | while | flops 54577152 | bytes 3427749 | solution.py:113
  375.7 2.8 pad_maximum_fusion
  (208 shorter events, 69.0 us)
Async XLA Ops:
  7.2 2.9 copy-start.6
  15.3 6.1 %copy-start.5 = (bf16[64,256]{1,0:T(8,128)(2,1)S(1)}, bf16[64,256]{1,0:T(8,128)(2,1)}, u32[]{:S(2)}) copy-start(bf16[64,256]{1,0:T(8,128)(2,1)} %param.15) | copy-start | bytes 98308
  15.3 15.3 %copy-start.10 = (s32[4]{0:T(128)S(1)}, s32[4]{0:T(128)}, u32[]{:S(2)}) copy-start(s32[4]{0:T(128)} %param.19) | copy-start | bytes 52
  15.3 16.8 %copy-start.3 = (bf16[512,256]{1,0:T(8,128)(2,1)S(1)}, bf16[512,256]{1,0:T(8,128)(2,1)}, u32[]{:S(2)}) copy-start(bf16[512,256]{1,0:T(8,128)(2,1)} %param.14) | copy-start | bytes 786436
  16.5 32.3 %collective-permute-start = (bf16[4096,16]{0,1:T(8,128)(2,1)}, bf16[4096,16]{0,1:T(8,128)(2,1)}, u32[]{:S(2)}, u32[]{:S(2)}) collective-permute-start(bf16[4096,16]{0,1:T(8,128)(2,1)} %get-tuple-element.371), channel_id=1, source_target_pairs={{0,1},{1,0},{2,3},{3,2},{4,5},{5,4},{6,7},{7,6},{8,9},{9,8},{10,11... | collective-permute-start | bytes 393224 | tf_op jit(solution)/shard_map/ppermute | solution.py:21
  17.0 36.3 %collective-permute-start.1 = (bf16[4096,16]{0,1:T(8,128)(2,1)}, bf16[4096,16]{0,1:T(8,128)(2,1)}, u32[]{:S(2)}, u32[]{:S(2)}) collective-permute-start(bf16[4096,16]{0,1:T(8,128)(2,1)} %get-tuple-element.370), channel_id=1, source_target_pairs={{0,2},{1,3},{2,0},{3,1},{4,6},{5,7},{6,4},{7,5},{8,10},{9,11},{10,... | collective-permute-start | bytes 393224 | tf_op jit(solution)/shard_map/ppermute | solution.py:21
  19.5 35.4 %collective-permute-start.2 = (bf16[4096,16]{0,1:T(8,128)(2,1)}, bf16[4096,16]{0,1:T(8,128)(2,1)}, u32[]{:S(2)}, u32[]{:S(2)}) collective-permute-start(bf16[4096,16]{0,1:T(8,128)(2,1)} %get-tuple-element.369), channel_id=1, source_target_pairs={{0,3},{1,2},{2,1},{3,0},{4,7},{5,6},{6,5},{7,4},{8,11},{9,10},{10,... | collective-permute-start | bytes 393224 | tf_op jit(solution)/shard_map/ppermute | solution.py:21
  19.6 39.2 %collective-permute-start.3 = (bf16[4096,16]{0,1:T(8,128)(2,1)}, bf16[4096,16]{0,1:T(8,128)(2,1)}, u32[]{:S(2)}, u32[]{:S(2)}) collective-permute-start(bf16[4096,16]{0,1:T(8,128)(2,1)} %get-tuple-element.368), channel_id=1, source_target_pairs={{0,4},{1,5},{2,6},{3,7},{4,0},{5,1},{6,2},{7,3},{8,12},{9,13},{10,... | collective-permute-start | bytes 393224 | tf_op jit(solution)/shard_map/ppermute | solution.py:21
  21.4 39.2 %collective-permute-start.4 = (bf16[4096,16]{0,1:T(8,128)(2,1)}, bf16[4096,16]{0,1:T(8,128)(2,1)}, u32[]{:S(2)}, u32[]{:S(2)}) collective-permute-start(bf16[4096,16]{0,1:T(8,128)(2,1)} %get-tuple-element.367), channel_id=1, source_target_pairs={{0,5},{1,4},{2,7},{3,6},{4,1},{5,0},{6,3},{7,2},{8,13},{9,12},{10,... | collective-permute-start | bytes 393224 | tf_op jit(solution)/shard_map/ppermute | solution.py:21
  24.5 13.8 %all-to-all-start.1 = ((bf16[16,2,512]{2,1,0:T(2,128)(2,1)}), bf16[16,2,512]{2,1,0:T(2,128)(2,1)S(1)}, u32[]{:S(2)}, u32[]{:S(2)}) async-start(bf16[16,2,512]{2,1,0:T(2,128)(2,1)} %reshape.446), calls=%async_computation.1 | async-start | bytes 65536 | tf_op jit(solution)/shard_map/all_to_all | solution.py:136
  33.4 3.8 copy-start.11
  34.2 26.4 %copy-start.4 = (bf16[4096,16]{0,1:T(8,128)(2,1)S(1)}, bf16[4096,16]{0,1:T(8,128)(2,1)}, u32[]{:S(2)}) copy-start(bf16[4096,16]{0,1:T(8,128)(2,1)} %get-tuple-element.362) | copy-start | bytes 393220
  34.5 1.3 copy-start.2
  38.3 84.4 %all-to-all-start = ((bf16[512,16,16]{0,2,1:T(8,128)(2,1)}), bf16[512,16,16]{0,2,1:T(8,128)(2,1)S(1)}, u32[]{:S(2)}, u32[]{:S(2)}) async-start(bf16[512,16,16]{0,2,1:T(8,128)(2,1)} %broadcast_select_fusion.1), calls=%async_computation | async-start | bytes 524288 | tf_op jit(solution)/shard_map/all_to_all | solution.py:129
  44.3 257.9 %all-gather.3.cloned.1.call-start = ((), (), s32[]{:S(2)}) async-start(), calls=%async_computation.2 | async-start | bytes 35651584 | tf_op jit(solution)/shard_map/all_gather | solution.py:28
  48.8 16.9 %collective-permute-start.5 = (bf16[4096,16]{0,1:T(8,128)(2,1)}, bf16[4096,16]{0,1:T(8,128)(2,1)S(1)}, u32[]{:S(2)}, u32[]{:S(2)}) collective-permute-start(bf16[4096,16]{0,1:T(8,128)(2,1)} %get-tuple-element.366), channel_id=1, source_target_pairs={{0,6},{1,7},{2,4},{3,5},{4,2},{5,3},{6,0},{7,1},{8,14},{9,15},{10,... | collective-permute-start | bytes 393224 | tf_op jit(solution)/shard_map/ppermute | solution.py:21
  53.3 13.2 %collective-permute-start.6 = (bf16[4096,16]{0,1:T(8,128)(2,1)}, bf16[4096,16]{0,1:T(8,128)(2,1)S(1)}, u32[]{:S(2)}, u32[]{:S(2)}) collective-permute-start(bf16[4096,16]{0,1:T(8,128)(2,1)} %get-tuple-element.365), channel_id=1, source_target_pairs={{0,7},{1,6},{2,5},{3,4},{4,3},{5,2},{6,1},{7,0},{8,15},{9,14},{10,... | collective-permute-start | bytes 393224 | tf_op jit(solution)/shard_map/ppermute | solution.py:21
  54.8 21.6 %collective-permute-start.7 = (bf16[4096,16]{0,1:T(8,128)(2,1)}, bf16[4096,16]{0,1:T(8,128)(2,1)S(1)}, u32[]{:S(2)}, u32[]{:S(2)}) collective-permute-start(bf16[4096,16]{0,1:T(8,128)(2,1)} %get-tuple-element.364), channel_id=1, source_target_pairs={{0,8},{1,9},{2,10},{3,11},{4,12},{5,13},{6,14},{7,15},{8,0},{9,1},... | collective-permute-start | bytes 393224 | tf_op jit(solution)/shard_map/ppermute | solution.py:21
  58.8 20.9 %collective-permute-start.8 = (bf16[4096,16]{0,1:T(8,128)(2,1)}, bf16[4096,16]{0,1:T(8,128)(2,1)S(1)}, u32[]{:S(2)}, u32[]{:S(2)}) collective-permute-start(bf16[4096,16]{0,1:T(8,128)(2,1)} %get-tuple-element.363), channel_id=1, source_target_pairs={{0,9},{1,8},{2,11},{3,10},{4,13},{5,12},{6,15},{7,14},{8,1},{9,0},... | collective-permute-start | bytes 393224 | tf_op jit(solution)/shard_map/ppermute | solution.py:21
  60.6 27.9 %collective-permute-start.9 = (bf16[4096,16]{0,1:T(8,128)(2,1)S(1)}, bf16[4096,16]{0,1:T(8,128)(2,1)S(1)}, u32[]{:S(2)}, u32[]{:S(2)}) collective-permute-start(bf16[4096,16]{0,1:T(8,128)(2,1)S(1)} %copy-done.4), channel_id=1, source_target_pairs={{0,10},{1,11},{2,8},{3,9},{4,14},{5,15},{6,12},{7,13},{8,2},{9,3},... | collective-permute-start | bytes 393224 | tf_op jit(solution)/shard_map/ppermute | solution.py:21
  65.7 26.1 %collective-permute-start.10 = (bf16[4096,16]{0,1:T(8,128)(2,1)S(1)}, bf16[4096,16]{0,1:T(8,128)(2,1)S(1)}, u32[]{:S(2)}, u32[]{:S(2)}) collective-permute-start(bf16[4096,16]{0,1:T(8,128)(2,1)S(1)} %get-tuple-element.361), channel_id=1, source_target_pairs={{0,11},{1,10},{2,9},{3,8},{4,15},{5,14},{6,13},{7,12},{8,3},{9,2},... | collective-permute-start | bytes 393224 | tf_op jit(solution)/shard_map/ppermute | solution.py:21
  66.4 26.1 %collective-permute-start.11 = (bf16[4096,16]{0,1:T(8,128)(2,1)S(1)}, bf16[4096,16]{0,1:T(8,128)(2,1)S(1)}, u32[]{:S(2)}, u32[]{:S(2)}) collective-permute-start(bf16[4096,16]{0,1:T(8,128)(2,1)S(1)} %get-tuple-element.360), channel_id=1, source_target_pairs={{0,12},{1,13},{2,14},{3,15},{4,8},{5,9},{6,10},{7,11},{8,4},{9,5},... | collective-permute-start | bytes 393224 | tf_op jit(solution)/shard_map/ppermute | solution.py:21
  76.4 16.8 %collective-permute-start.12 = (bf16[4096,16]{0,1:T(8,128)(2,1)S(1)}, bf16[4096,16]{0,1:T(8,128)(2,1)S(1)}, u32[]{:S(2)}, u32[]{:S(2)}) collective-permute-start(bf16[4096,16]{0,1:T(8,128)(2,1)S(1)} %get-tuple-element.359), channel_id=1, source_target_pairs={{0,13},{1,12},{2,15},{3,14},{4,9},{5,8},{6,11},{7,10},{8,5},{9,4},... | collective-permute-start | bytes 393224 | tf_op jit(solution)/shard_map/ppermute | solution.py:21
  79.7 18.2 %collective-permute-start.13 = (bf16[4096,16]{0,1:T(8,128)(2,1)S(1)}, bf16[4096,16]{0,1:T(8,128)(2,1)S(1)}, u32[]{:S(2)}, u32[]{:S(2)}) collective-permute-start(bf16[4096,16]{0,1:T(8,128)(2,1)S(1)} %get-tuple-element.358), channel_id=1, source_target_pairs={{0,14},{1,15},{2,12},{3,13},{4,10},{5,11},{6,8},{7,9},{8,6},{9,7},... | collective-permute-start | bytes 393224 | tf_op jit(solution)/shard_map/ppermute | solution.py:21
  88.5 21.0 %collective-permute-start.14 = (bf16[4096,16]{0,1:T(8,128)(2,1)S(1)}, bf16[4096,16]{0,1:T(8,128)(2,1)S(1)}, u32[]{:S(2)}, u32[]{:S(2)}) collective-permute-start(bf16[4096,16]{0,1:T(8,128)(2,1)S(1)} %get-tuple-element.357), channel_id=1, source_target_pairs={{0,15},{1,14},{2,13},{3,12},{4,11},{5,10},{6,9},{7,8},{8,7},{9,6},... | collective-permute-start | bytes 393224 | tf_op jit(solution)/shard_map/ppermute | solution.py:21
  122.7 1.0 copy-start.1
  124.1 1.3 copy-start
  127.1 0.7 copy-start.9
  127.1 1.3 copy-start.12
  344.0 2.3 copy-start.7
  346.3 17.8 %copy-start.8 = (f32[64]{0:T(128)S(1)}, f32[64]{0:T(128)}, u32[]{:S(2)}) copy-start(f32[64]{0:T(128)} %get-tuple-element.354) | copy-start | bytes 772
Sparse Core Ops, SparseCore 0:
  127.2 174.9 all-gather.2
